TPU v7x, 256 devices: a whole 4x4x8 slice. The times are simulated.
256 devices in a mesh: row: 8 (over x, core), col: 32 (over y, z).
Axes of the slice: x: 4, y: 4, z: 8, core: 2. Of those that a mesh axis runs over, the one named last changes fastest.
Arguments:
- factor: float32 [6, 8, 32, 512, 512], P(None, 'row', 'col'), may hold values from -0.1875 to 0.1875
- rhs: float32 [6, 8, 32, 128, 128], P(None, 'row', 'col'), may hold values from -6 to 6
- inverses: float32 [4, 512, 512], replicated, may hold values from -0.5 to 2, as said below
Outputs:
- solved: float32 [4, 512, 128], P(None, 'col')
- remaining: float32 [6, 8, 32, 128, 128], P(None, 'row', 'col')
Inputs may be any that keep to these rules, and one draw needn't show every extreme that they name: `inverses`: each block is lower triangular with its diagonal between 0.5 and 2 and entries below it of magnitude at most 4 / sqrt(512).
All inputs are finite; a program needn't handle non-finite values.
Results may differ from a plain program's by a relative error of at most 0.00011.
Values sent between devices are 32-bit elements; how exact they have to be, the bound alone decides.
A program may use at most 64 MiB of HBM per device.

v0:
```python
import jax
import jax.numpy as jnp
from jax import lax
from jax.sharding import PartitionSpec as P


def shifted(block, axis, distance):
    devices = range(lax.axis_size(axis))
    route = [((i - distance) % len(devices), i) for i in devices]
    return lax.ppermute(block, axis, route)


def broadcast(x, axis, root):
    mine = lax.axis_index(axis) == root
    return lax.psum(jnp.where(mine, x, jnp.zeros_like(x)), axis)


def group_reduce(update, member, steps, groups):
    blocks = update.shape[0]
    nrhs = update.shape[2]
    split = update.reshape(blocks, steps, update.shape[1] // steps, nrhs)
    total = lax.dynamic_index_in_dim(split, member, 1, keepdims=False)
    for offset in range(1, steps):
        piece = lax.dynamic_index_in_dim(split, (member + offset) % steps, 1, keepdims=False)
        total = total + shifted(piece, "col", offset * groups)
    return total


def on_device(factor, rhs, inverses):
    steps = inverses.shape[0]
    blocks = factor.shape[0]
    width = factor.shape[3]
    quarter = rhs.shape[3]
    nrhs = rhs.shape[4]
    row_count = lax.axis_size("row")
    col_count = lax.axis_size("col")
    groups = col_count // steps
    row_pos = lax.axis_index("row")
    col_pos = lax.axis_index("col")
    member = col_pos // groups
    group = col_pos % groups
    block_ids = (jnp.arange(blocks, dtype=jnp.int32) * row_count + row_pos) * groups + group
    panel = factor[:, 0, 0]
    current = rhs[:, 0, 0]
    solved_list = []
    for k in range(steps):
        owner_row = k // groups
        owner_group = k % groups
        placed = lax.dynamic_update_slice(
            jnp.zeros((width, nrhs), jnp.float32),
            current[0],
            (member * quarter, jnp.zeros((), jnp.int32)),
        )
        contrib = placed
        is_owner = jnp.logical_and(row_pos == owner_row, group == owner_group)
        contrib = jnp.where(is_owner, contrib, jnp.zeros_like(contrib))
        complete = lax.psum(contrib, "col")
        solved_block = jnp.dot(inverses[k], complete, precision=lax.Precision.HIGHEST)
        solved_block = broadcast(solved_block, "row", owner_row)
        solved_list.append(solved_block)
        keep = (block_ids > k).astype(jnp.float32)[:, None, None]

        def column_update(solved_now=solved_block, keep_now=keep):
            return (
                jnp.einsum("rji,jh->rih", panel, solved_now, precision=lax.Precision.HIGHEST)
                * keep_now
            )

        def no_update():
            return jnp.zeros((blocks, width, nrhs), jnp.float32)

        update = lax.cond(member == k, column_update, no_update)
        current = current - group_reduce(update, member, steps, groups)
    stacked = jnp.stack(solved_list)
    share = width // col_count
    solved_rows = lax.dynamic_slice_in_dim(stacked, col_pos * share, share, 1)
    return (solved_rows, current[:, None, None])


def solution(mesh):
    in_specs = (P(None, "row", "col", None, None), P(None, "row", "col", None, None), P())
    out_specs = (P(None, "col", None), P(None, "row", "col", None, None))
    return jax.shard_map(
        on_device, mesh=mesh, in_specs=in_specs, out_specs=out_specs, check_vma=False
    )
```

profile of v0, /device:TPU:7, one launch (start us, length us, event | category | flops | bytes accessed | tf_op | source)
XLA Modules:
  0.0 980.9 jit_solution(4131290574086656395)
XLA Ops:
  7.2 0.0 all-reduce.9.cloned.1.call-start
  7.3 0.9 bitcast_dynamic-update-slice_fusion
  8.1 0.7 copy-done.5
  8.9 0.0 all-reduce.11.cloned.1.call-start
  9.0 6.6 copy.5
  15.6 139.2 %all-reduce.9.cloned.1.call-done = f32[512,128]{1,0:T(8,128)} async-done(((f32[512,128]{1,0:T(8,128)}), f32[512,128]{1,0:T(8,128)}) %all-reduce.9.cloned.1.call-update) | async-done | bytes 262160 | tf_op jit(solution)/shard_map/psum | solution.py:57
  154.7 3.3 fusion.7
  158.0 0.0 all-reduce.11.cloned.1.call-update
  158.0 0.0 all-reduce.13.cloned.1.call-start
  158.1 65.0 %all-reduce.11.cloned.1.call-done = f32[512,128]{0,1:T(8,128)} async-done(((f32[512,128]{0,1:T(8,128)}), f32[512,128]{0,1:T(8,128)}) %all-reduce.11.cloned.1.call-update) | async-done | bytes 262160 | tf_op jit(solution)/shard_map/psum | solution.py:15
  223.1 7.2 conditional.4
  223.1 7.2 convolution_multiply_fusion
  230.3 0.9 dynamic-slice_bitcast_fusion.11
  231.2 2.7 collective-permute-start.2
  233.8 18.1 %collective-permute-done = f32[6,128,128]{2,1,0:T(8,128)S(1)} collective-permute-done((f32[6,128,128]{2,1,0:T(8,128)}, f32[6,128,128]{2,1,0:T(8,128)S(1)}, u32[]{:S(2)}, u32[]{:S(2)}) %collective-permute-start) | collective-permute-done | bytes 393248 | tf_op jit(solution)/shard_map/ppermute | solution.py:10
  251.9 0.3 collective-permute-done.2
  252.2 1.1 fusion.28
  253.4 0.7 copy-done.6
  254.0 0.0 all-reduce.13.cloned.1.call-update
  254.1 0.0 all-reduce.15.cloned.1.call-start
  254.1 140.4 %all-reduce.13.cloned.1.call-done = f32[512,128]{1,0:T(8,128)} async-done(((f32[512,128]{1,0:T(8,128)}), f32[512,128]{1,0:T(8,128)}) %all-reduce.13.cloned.1.call-update) | async-done | bytes 262160 | tf_op jit(solution)/shard_map/psum | solution.py:57
  394.5 3.3 fusion.6
  397.8 0.0 all-reduce.17.cloned.1.call-start
  397.8 65.0 %all-reduce.15.cloned.1.call-done = f32[512,128]{0,1:T(8,128)} async-done(((f32[512,128]{0,1:T(8,128)}), f32[512,128]{0,1:T(8,128)}) %all-reduce.15.cloned.1.call-update) | async-done | bytes 262160 | tf_op jit(solution)/shard_map/psum | solution.py:15
  462.9 0.2 conditional.5
  462.9 0.2 reshape.83
  463.1 0.9 dynamic-slice_bitcast_fusion.8
  463.9 8.2 collective-permute-start.3
  472.1 2.4 collective-permute-start.5
  474.5 6.6 collective-permute-done.3
  481.1 8.3 collective-permute-done.4
  489.4 0.8 collective-permute-done.5
  490.3 1.1 fusion.25
  491.4 0.7 copy-done.7
  492.2 0.0 all-reduce.19.cloned.1.call-start
  492.2 141.5 %all-reduce.17.cloned.1.call-done = f32[512,128]{1,0:T(8,128)} async-done(((f32[512,128]{1,0:T(8,128)}), f32[512,128]{1,0:T(8,128)}) %all-reduce.17.cloned.1.call-update) | async-done | bytes 262160 | tf_op jit(solution)/shard_map/psum | solution.py:57
  633.7 3.3 fusion.5
  637.0 0.0 all-reduce.21.cloned.1.call-start
  637.0 65.1 %all-reduce.19.cloned.1.call-done = f32[512,128]{0,1:T(8,128)} async-done(((f32[512,128]{0,1:T(8,128)}), f32[512,128]{0,1:T(8,128)}) %all-reduce.19.cloned.1.call-update) | async-done | bytes 262160 | tf_op jit(solution)/shard_map/psum | solution.py:15
  702.1 0.2 conditional.6
  702.1 0.2 reshape.85
  702.3 0.9 dynamic-slice_bitcast_fusion.5
  703.1 1.2 collective-permute-start.6
  704.3 8.5 collective-permute-start.7
  712.9 2.1 collective-permute-start.8
  714.9 0.5 collective-permute-done.6
  715.4 15.7 %collective-permute-done.7 = f32[6,128,128]{2,1,0:T(8,128)S(1)} collective-permute-done((f32[6,128,128]{2,1,0:T(8,128)S(1)}, f32[6,128,128]{2,1,0:T(8,128)S(1)}, u32[]{:S(2)}, u32[]{:S(2)}) %collective-permute-start.7) | collective-permute-done | bytes 393248 | tf_op jit(solution)/shard_map/ppermute | solution.py:10
  731.1 1.1 fusion.22
  732.3 0.7 copy-done.4
  733.0 0.0 all-reduce.23.cloned.1.call-start
  733.0 141.1 %all-reduce.21.cloned.1.call-done = f32[512,128]{1,0:T(8,128)} async-done(((f32[512,128]{1,0:T(8,128)}), f32[512,128]{1,0:T(8,128)}) %all-reduce.21.cloned.1.call-update) | async-done | bytes 262160 | tf_op jit(solution)/shard_map/psum | solution.py:57
  874.1 3.3 fusion.4
  877.4 65.1 %all-reduce.23.cloned.1.call-done = f32[512,128]{0,1:T(8,128)} async-done(((f32[512,128]{0,1:T(8,128)}), f32[512,128]{0,1:T(8,128)}) %all-reduce.23.cloned.1.call-update) | async-done | bytes 262160 | tf_op jit(solution)/shard_map/psum | solution.py:15
  942.5 0.2 conditional.7
  942.5 0.2 reshape.87
  942.7 1.1 dynamic-slice_bitcast_fusion.2
  943.8 2.7 collective-permute-start.10
  946.5 6.7 collective-permute-start.11
  953.2 0.6 collective-permute-start.9
  953.8 0.1 fusion.31
  954.0 0.7 copy.10
  954.7 1.8 collective-permute-done.10
  956.5 15.5 %collective-permute-done.11 = f32[6,128,128]{2,1,0:T(8,128)} collective-permute-done((f32[6,128,128]{2,1,0:T(8,128)}, f32[6,128,128]{2,1,0:T(8,128)}, u32[]{:S(2)}, u32[]{:S(2)}) %collective-permute-start.11) | collective-permute-done | bytes 393248 | tf_op jit(solution)/shard_map/ppermute | solution.py:10
  972.0 2.1 fusion.19
  (35 shorter events, 0.3 us)
Async XLA Ops:
  7.2 147.6 %all-reduce.9.cloned.1.call-start = ((), (), s32[]{:S(2)}) async-start(), calls=%async_computation | async-start | bytes 524288 | tf_op jit(solution)/shard_map/psum | solution.py:57
  8.1 0.7 copy-start.5
  8.9 214.3 %all-reduce.11.cloned.1.call-start = ((), (), s32[]{:S(2)}) async-start(), calls=%async_computation.1 | async-start | bytes 524288 | tf_op jit(solution)/shard_map/psum | solution.py:15
  158.0 236.5 %all-reduce.13.cloned.1.call-start = ((), (), s32[]{:S(2)}) async-start(), calls=%async_computation.2 | async-start | bytes 524288 | tf_op jit(solution)/shard_map/psum | solution.py:57
  230.3 21.9 %copy-start.8 = (f32[6,1,1,128,128]{4,3,2,1,0:T(8,128)S(1)}, f32[6,1,1,128,128]{4,3,2,1,0:T(8,128)}, u32[]{:S(2)}) copy-start(f32[6,1,1,128,128]{4,3,2,1,0:T(8,128)} %param.12) | copy-start | bytes 1179652
  231.1 20.7 %collective-permute-start = (f32[6,128,128]{2,1,0:T(8,128)}, f32[6,128,128]{2,1,0:T(8,128)S(1)}, u32[]{:S(2)}, u32[]{:S(2)}) collective-permute-start(f32[6,128,128]{2,1,0:T(8,128)} %get-tuple-element.79), channel_id=1, source_target_pairs={{24,0},{25,1},{26,2},{27,3},{28,4},{29,5},{30,6},{31,7},{0,8},{1,9... | collective-permute-start | bytes 1179656 | tf_op jit(solution)/shard_map/ppermute | solution.py:10
  231.1 20.7 %collective-permute-start.1 = (f32[6,128,128]{2,1,0:T(8,128)S(1)}, f32[6,128,128]{2,1,0:T(8,128)S(1)}, u32[]{:S(2)}, u32[]{:S(2)}) collective-permute-start(f32[6,128,128]{2,1,0:T(8,128)S(1)} %get-tuple-element.81), channel_id=1, source_target_pairs={{16,0},{17,1},{18,2},{19,3},{20,4},{21,5},{22,6},{23,7},{24,8},{25... | collective-permute-start | bytes 1179656 | tf_op jit(solution)/shard_map/ppermute | solution.py:10
  231.2 21.0 %collective-permute-start.2 = (f32[6,128,128]{2,1,0:T(8,128)S(1)}, f32[6,128,128]{2,1,0:T(8,128)}, u32[]{:S(2)}, u32[]{:S(2)}) collective-permute-start(f32[6,128,128]{2,1,0:T(8,128)S(1)} %get-tuple-element.80), channel_id=1, source_target_pairs={{8,0},{9,1},{10,2},{11,3},{12,4},{13,5},{14,6},{15,7},{16,8},{17,9... | collective-permute-start | bytes 1179656 | tf_op jit(solution)/shard_map/ppermute | solution.py:10
  253.3 0.7 copy-start.6
  254.1 208.8 %all-reduce.15.cloned.1.call-start = ((), (), s32[]{:S(2)}) async-start(), calls=%async_computation.3 | async-start | bytes 524288 | tf_op jit(solution)/shard_map/psum | solution.py:15
  397.8 235.9 %all-reduce.17.cloned.1.call-start = ((), (), s32[]{:S(2)}) async-start(), calls=%async_computation.4 | async-start | bytes 524288 | tf_op jit(solution)/shard_map/psum | solution.py:57
  463.9 17.2 %collective-permute-start.3 = (f32[6,128,128]{2,1,0:T(8,128)}, f32[6,128,128]{2,1,0:T(8,128)S(1)}, u32[]{:S(2)}, u32[]{:S(2)}) collective-permute-start(f32[6,128,128]{2,1,0:T(8,128)} %get-tuple-element.76), channel_id=1, source_target_pairs={{24,0},{25,1},{26,2},{27,3},{28,4},{29,5},{30,6},{31,7},{0,8},{1,9... | collective-permute-start | bytes 1179656 | tf_op jit(solution)/shard_map/ppermute | solution.py:10
  472.1 17.3 %collective-permute-start.4 = (f32[6,128,128]{2,1,0:T(8,128)S(1)}, f32[6,128,128]{2,1,0:T(8,128)S(1)}, u32[]{:S(2)}, u32[]{:S(2)}) collective-permute-start(f32[6,128,128]{2,1,0:T(8,128)S(1)} %get-tuple-element.78), channel_id=1, source_target_pairs={{16,0},{17,1},{18,2},{19,3},{20,4},{21,5},{22,6},{23,7},{24,8},{25... | collective-permute-start | bytes 1179656 | tf_op jit(solution)/shard_map/ppermute | solution.py:10
  472.1 18.2 %collective-permute-start.5 = (f32[6,128,128]{2,1,0:T(8,128)S(1)}, f32[6,128,128]{2,1,0:T(8,128)}, u32[]{:S(2)}, u32[]{:S(2)}) collective-permute-start(f32[6,128,128]{2,1,0:T(8,128)S(1)} %get-tuple-element.77), channel_id=1, source_target_pairs={{8,0},{9,1},{10,2},{11,3},{12,4},{13,5},{14,6},{15,7},{16,8},{17,9... | collective-permute-start | bytes 1179656 | tf_op jit(solution)/shard_map/ppermute | solution.py:10
  491.4 0.7 copy-start.7
  492.2 209.9 %all-reduce.19.cloned.1.call-start = ((), (), s32[]{:S(2)}) async-start(), calls=%async_computation.5 | async-start | bytes 524288 | tf_op jit(solution)/shard_map/psum | solution.py:15
  637.0 237.1 %all-reduce.21.cloned.1.call-start = ((), (), s32[]{:S(2)}) async-start(), calls=%async_computation.6 | async-start | bytes 524288 | tf_op jit(solution)/shard_map/psum | solution.py:57
  703.1 12.3 %collective-permute-start.6 = (f32[6,128,128]{2,1,0:T(8,128)}, f32[6,128,128]{2,1,0:T(8,128)S(1)}, u32[]{:S(2)}, u32[]{:S(2)}) collective-permute-start(f32[6,128,128]{2,1,0:T(8,128)} %get-tuple-element.73), channel_id=1, source_target_pairs={{24,0},{25,1},{26,2},{27,3},{28,4},{29,5},{30,6},{31,7},{0,8},{1,9... | collective-permute-start | bytes 1179656 | tf_op jit(solution)/shard_map/ppermute | solution.py:10
  704.3 26.8 %collective-permute-start.7 = (f32[6,128,128]{2,1,0:T(8,128)S(1)}, f32[6,128,128]{2,1,0:T(8,128)S(1)}, u32[]{:S(2)}, u32[]{:S(2)}) collective-permute-start(f32[6,128,128]{2,1,0:T(8,128)S(1)} %get-tuple-element.75), channel_id=1, source_target_pairs={{16,0},{17,1},{18,2},{19,3},{20,4},{21,5},{22,6},{23,7},{24,8},{25... | collective-permute-start | bytes 1179656 | tf_op jit(solution)/shard_map/ppermute | solution.py:10
  712.9 18.2 %collective-permute-start.8 = (f32[6,128,128]{2,1,0:T(8,128)S(1)}, f32[6,128,128]{2,1,0:T(8,128)}, u32[]{:S(2)}, u32[]{:S(2)}) collective-permute-start(f32[6,128,128]{2,1,0:T(8,128)S(1)} %get-tuple-element.74), channel_id=1, source_target_pairs={{8,0},{9,1},{10,2},{11,3},{12,4},{13,5},{14,6},{15,7},{16,8},{17,9... | collective-permute-start | bytes 1179656 | tf_op jit(solution)/shard_map/ppermute | solution.py:10
  732.2 0.7 copy-start.4
  733.0 209.5 %all-reduce.23.cloned.1.call-start = ((), (), s32[]{:S(2)}) async-start(), calls=%async_computation.7 | async-start | bytes 524288 | tf_op jit(solution)/shard_map/psum | solution.py:15
  942.7 11.1 %copy-start = (f32[512,128]{0,1:T(8,128)S(1)}, f32[512,128]{0,1:T(8,128)}, u32[]{:S(2)}) copy-start(f32[512,128]{0,1:T(8,128)} %all-reduce.11.cloned.1.call-done) | copy-start | bytes 786436
  942.7 11.1 %copy-start.1 = (f32[512,128]{0,1:T(8,128)S(1)}, f32[512,128]{0,1:T(8,128)}, u32[]{:S(2)}) copy-start(f32[512,128]{0,1:T(8,128)} %all-reduce.15.cloned.1.call-done) | copy-start | bytes 786436
  942.7 11.1 %copy-start.2 = (f32[512,128]{0,1:T(8,128)S(1)}, f32[512,128]{0,1:T(8,128)}, u32[]{:S(2)}) copy-start(f32[512,128]{0,1:T(8,128)} %all-reduce.19.cloned.1.call-done) | copy-start | bytes 786436
  942.7 11.1 %copy-start.3 = (f32[512,128]{0,1:T(8,128)S(1)}, f32[512,128]{0,1:T(8,128)}, u32[]{:S(2)}) copy-start(f32[512,128]{0,1:T(8,128)} %all-reduce.23.cloned.1.call-done) | copy-start | bytes 786436
  943.8 12.7 %collective-permute-start.10 = (f32[6,128,128]{2,1,0:T(8,128)}, f32[6,128,128]{2,1,0:T(8,128)}, u32[]{:S(2)}, u32[]{:S(2)}) collective-permute-start(f32[6,128,128]{2,1,0:T(8,128)} %get-tuple-element.72), channel_id=1, source_target_pairs={{16,0},{17,1},{18,2},{19,3},{20,4},{21,5},{22,6},{23,7},{24,8},{25... | collective-permute-start | bytes 1179656 | tf_op jit(solution)/shard_map/ppermute | solution.py:10
  946.5 25.5 %collective-permute-start.11 = (f32[6,128,128]{2,1,0:T(8,128)}, f32[6,128,128]{2,1,0:T(8,128)}, u32[]{:S(2)}, u32[]{:S(2)}) collective-permute-start(f32[6,128,128]{2,1,0:T(8,128)} %get-tuple-element.71), channel_id=1, source_target_pairs={{8,0},{9,1},{10,2},{11,3},{12,4},{13,5},{14,6},{15,7},{16,8},{17,9... | collective-permute-start | bytes 1179656 | tf_op jit(solution)/shard_map/ppermute | solution.py:10
  953.2 18.8 %collective-permute-start.9 = (f32[6,128,128]{2,1,0:T(8,128)}, f32[6,128,128]{2,1,0:T(8,128)}, u32[]{:S(2)}, u32[]{:S(2)}) collective-permute-start(f32[6,128,128]{2,1,0:T(8,128)} %get-tuple-element.70), channel_id=1, source_target_pairs={{24,0},{25,1},{26,2},{27,3},{28,4},{29,5},{30,6},{31,7},{0,8},{1,9... | collective-permute-start | bytes 1179656 | tf_op jit(solution)/shard_map/ppermute | solution.py:10
Sparse Core Ops, SparseCore 0:
  12.0 142.6 all-reduce.8
  158.1 64.9 all-reduce.10
  254.2 140.2 all-reduce.12
  397.9 64.9 all-reduce.14
  492.3 141.3 all-reduce.16
  637.1 64.9 all-reduce.18
  733.1 140.9 all-reduce.20
  877.5 64.9 all-reduce.22
where the time goes:
time: 981 us
  waiting for transfers between devices  890 us (91%)
  starting transfers between devices  35.4 us (4%)
  matrix products  20.2 us (2%)
  between operations  14.4 us (1%)
  local copies, waits for them, and re-layouts  14.3 us (1%)
    psum x4, waiting for transfers between devices, on_device(): complete = lax.psum(contrib, 'col')  562 us
    psum x4, waiting for transfers between devices, broadcast(): return lax.psum(jnp.where(mine, x, jnp.zeros_like(x)), axis)  260 us
    ppermute x12, waiting for transfers between devices, shifted(): return lax.ppermute(block, axis, route)  67.6 us
    ppermute x12, starting transfers between devices, shifted(): return lax.ppermute(block, axis, route)  35.1 us
  transfers between devices with their start and end apart: 20, of which 17 were waited for; matrix products, arithmetic and copies ran while one was open for 1% of the time, Pallas kernels for 0%

commit v1 on v0

--- a/solution.py
+++ b/solution.py
@@ -12,7 +12,7 @@
 
 def broadcast(x, axis, root):
     mine = lax.axis_index(axis) == root
-    return lax.psum(jnp.where(mine, x, jnp.zeros_like(x)), axis)
+    return jnp.sum(lax.all_gather(jnp.where(mine, x, jnp.zeros_like(x)), axis), axis=0)
 
 
 def group_reduce(update, member, steps, groups):

time: 981 us -> 855 us (0.87)
  waiting for transfers between devices: 890 us -> 745 us
  local copies, waits for them, and re-layouts: 14.3 us -> 27.6 us
    psum x4 -> x0, waiting for transfers between devices: 260 us -> none  [broadcast(): return lax.psum(jnp.where(mine, x, jnp.zeros_like(x)), axis)]
    all_gather x0 -> x4, waiting for transfers between devices: none -> 108 us  [broadcast(): lax.all_gather(jnp.where(mine, x, jnp.zeros_like(x)), axis)]
    unnamed x20 -> x18, local copies, waits for them, and re-layouts: 10.1 us -> 23 us
  transfers between devices with their start and end apart: 20 -> 20, of which waited for: 17 -> 16; matrix products, arithmetic and copies ran while one was open for 1% -> 1% of each run, Pallas kernels for 0% -> 0%
where the time goes in v1:
time: 855 us; the launch traced here: 852 us
  waiting for transfers between devices  745 us (87%)
  starting transfers between devices  35.6 us (4%)
  local copies, waits for them, and re-layouts  27.6 us (3%)
  matrix products  20.2 us (2%)
  between operations  14.4 us (2%)
  other arithmetic  9.02 us (1%)
    psum x4, waiting for transfers between devices, on_device(): complete = lax.psum(contrib, 'col')  571 us
    all_gather x4, waiting for transfers between devices, broadcast(): lax.all_gather(jnp.where(mine, x, jnp.zeros_like(x)), axis)  108 us
    ppermute x12, waiting for transfers between devices, shifted(): return lax.ppermute(block, axis, route)  66.6 us
    ppermute x12, starting transfers between devices, shifted(): return lax.ppermute(block, axis, route)  35.1 us
    unnamed x18, local copies, waits for them, and re-layouts  23 us
  transfers between devices with their start and end apart: 20, of which 16 were waited for; matrix products, arithmetic and copies ran while one was open for 1% of the time, Pallas kernels for 0%

profile of v1, /device:TPU:7, one launch (start us, length us, event | category | flops | bytes accessed | tf_op | source)
XLA Modules:
  0.0 852.5 jit_solution(14651620832224271785)
XLA Ops:
  7.3 0.9 bitcast_dynamic-update-slice_fusion
  8.1 0.7 copy-done.1
  8.9 0.0 all-gather.9.cloned.1.call-start
  8.9 145.8 %all-reduce.5.cloned.1.call-done = f32[512,128]{1,0:T(8,128)} async-done(((f32[512,128]{1,0:T(8,128)}), f32[512,128]{1,0:T(8,128)}) %all-reduce.5.cloned.1.call-update) | async-done | bytes 262160 | tf_op jit(solution)/shard_map/psum | solution.py:57
  154.7 3.3 fusion.7
  158.1 6.6 copy.6
  164.7 22.0 %all-gather.9.cloned.1.call-done = f32[4096,128]{0,1:T(8,128)} async-done(((f32[512,128]{0,1:T(8,128)}), f32[4096,128]{0,1:T(8,128)}) %all-gather.9.cloned.1.call-update) | async-done | bytes 2097168 | tf_op jit(solution)/shard_map/all_gather | solution.py:15
  186.7 3.2 copy.20
  189.9 0.5 bitcast_reduce_fusion.3
  190.5 7.2 conditional.4
  190.5 7.2 convolution_multiply_fusion
  197.7 1.0 dynamic-slice_bitcast_fusion.11
  198.7 2.7 collective-permute-start.2
  201.4 17.6 %collective-permute-done = f32[6,128,128]{2,1,0:T(8,128)S(1)} collective-permute-done((f32[6,128,128]{2,1,0:T(8,128)}, f32[6,128,128]{2,1,0:T(8,128)S(1)}, u32[]{:S(2)}, u32[]{:S(2)}) %collective-permute-start) | collective-permute-done | bytes 393248 | tf_op jit(solution)/shard_map/ppermute | solution.py:10
  219.0 0.5 collective-permute-done.2
  219.4 1.2 fusion.28
  220.7 0.7 copy-done.2
  221.5 140.9 %all-reduce.7.cloned.1.call-done = f32[512,128]{1,0:T(8,128)} async-done(((f32[512,128]{1,0:T(8,128)}), f32[512,128]{1,0:T(8,128)}) %all-reduce.7.cloned.1.call-update) | async-done | bytes 262160 | tf_op jit(solution)/shard_map/psum | solution.py:57
  362.4 3.3 fusion.6
  365.7 0.2 all-reduce.9.cloned.1.call-start
  365.9 28.5 %all-gather.11.cloned.1.call-done = f32[4096,128]{0,1:T(8,128)} async-done(((f32[512,128]{0,1:T(8,128)}), f32[4096,128]{0,1:T(8,128)}) %all-gather.11.cloned.1.call-update) | async-done | bytes 2097168 | tf_op jit(solution)/shard_map/all_gather | solution.py:15
  394.4 3.2 copy.21
  397.6 0.5 bitcast_reduce_fusion.2
  398.2 0.2 conditional.5
  398.2 0.2 reshape.83
  398.4 1.0 dynamic-slice_bitcast_fusion.8
  399.4 8.2 collective-permute-start.3
  407.6 2.4 collective-permute-start.5
  410.0 6.2 collective-permute-done.3
  416.1 8.4 collective-permute-done.4
  424.5 1.1 collective-permute-done.5
  425.6 1.2 fusion.25
  426.9 0.7 copy-done.3
  427.7 142.1 %all-reduce.9.cloned.1.call-done = f32[512,128]{1,0:T(8,128)} async-done(((f32[512,128]{1,0:T(8,128)}), f32[512,128]{1,0:T(8,128)}) %all-reduce.9.cloned.1.call-update) | async-done | bytes 262160 | tf_op jit(solution)/shard_map/psum | solution.py:57
  569.7 3.3 fusion.5
  573.1 28.7 %all-gather.13.cloned.1.call-done = f32[4096,128]{0,1:T(8,128)} async-done(((f32[512,128]{0,1:T(8,128)}), f32[4096,128]{0,1:T(8,128)}) %all-gather.13.cloned.1.call-update) | async-done | bytes 2097168 | tf_op jit(solution)/shard_map/all_gather | solution.py:15
  601.7 3.2 copy.22
  605.0 0.5 bitcast_reduce_fusion.1
  605.5 0.4 conditional.6
  605.5 0.2 reshape.85
  605.9 1.0 dynamic-slice_bitcast_fusion.5
  607.0 1.2 collective-permute-start.6
  608.2 8.5 %collective-permute-start.7 = (f32[6,128,128]{2,1,0:T(8,128)}, f32[6,128,128]{2,1,0:T(8,128)}, u32[]{:S(2)}, u32[]{:S(2)}) collective-permute-start(f32[6,128,128]{2,1,0:T(8,128)} %get-tuple-element.75), channel_id=1, source_target_pairs={{16,0},{17,1},{18,2},{19,3},{20,4},{21,5},{22,6},{23,7},{24,8},{25... | collective-permute-start | bytes 1179656 | tf_op jit(solution)/shard_map/ppermute | solution.py:10
  616.7 2.1 collective-permute-start.8
  618.8 0.0 collective-permute-done.6
  618.8 15.9 %collective-permute-done.7 = f32[6,128,128]{2,1,0:T(8,128)} collective-permute-done((f32[6,128,128]{2,1,0:T(8,128)}, f32[6,128,128]{2,1,0:T(8,128)}, u32[]{:S(2)}, u32[]{:S(2)}) %collective-permute-start.7) | collective-permute-done | bytes 393248 | tf_op jit(solution)/shard_map/ppermute | solution.py:10
  634.7 1.3 fusion.22
  636.1 0.7 copy-done
  636.9 141.8 %all-reduce.11.cloned.1.call-done = f32[512,128]{1,0:T(8,128)} async-done(((f32[512,128]{1,0:T(8,128)}), f32[512,128]{1,0:T(8,128)}) %all-reduce.11.cloned.1.call-update) | async-done | bytes 262160 | tf_op jit(solution)/shard_map/psum | solution.py:57
  778.7 3.3 fusion.4
  782.0 28.7 %all-gather.15.cloned.1.call-done = f32[4096,128]{0,1:T(8,128)} async-done(((f32[512,128]{0,1:T(8,128)}), f32[4096,128]{0,1:T(8,128)}) %all-gather.15.cloned.1.call-update) | async-done | bytes 2097168 | tf_op jit(solution)/shard_map/all_gather | solution.py:15
  810.7 3.2 copy.23
  814.0 0.5 bitcast_reduce_fusion
  814.5 0.2 conditional.7
  814.5 0.2 reshape.87
  814.7 1.1 dynamic-slice_bitcast_fusion.2
  815.8 2.7 collective-permute-start.10
  818.5 6.7 collective-permute-start.11
  825.2 0.6 collective-permute-start.9
  825.8 0.1 fusion.31
  825.9 0.7 copy.11
  826.7 1.3 collective-permute-done.10
  828.0 15.6 %collective-permute-done.11 = f32[6,128,128]{2,1,0:T(8,128)} collective-permute-done((f32[6,128,128]{2,1,0:T(8,128)}, f32[6,128,128]{2,1,0:T(8,128)}, u32[]{:S(2)}, u32[]{:S(2)}) %collective-permute-start.11) | collective-permute-done | bytes 393248 | tf_op jit(solution)/shard_map/ppermute | solution.py:10
  843.6 2.1 fusion.19
  (37 shorter events, 0.5 us)
Async XLA Ops:
  7.2 147.6 %all-reduce.5.cloned.1.call-start = ((), (), s32[]{:S(2)}) async-start(), calls=%async_computation | async-start | bytes 524288 | tf_op jit(solution)/shard_map/psum | solution.py:57
  8.1 0.7 copy-start.1
  8.9 177.9 %all-gather.9.cloned.1.call-start = ((), (), s32[]{:S(2)}) async-start(), calls=%async_computation.4 | async-start | bytes 2359296 | tf_op jit(solution)/shard_map/all_gather | solution.py:15
  158.0 204.4 %all-reduce.7.cloned.1.call-start = ((), (), s32[]{:S(2)}) async-start(), calls=%async_computation.1 | async-start | bytes 524288 | tf_op jit(solution)/shard_map/psum | solution.py:57
  197.7 21.8 %copy-start.4 = (f32[6,1,1,128,128]{4,3,2,1,0:T(8,128)S(1)}, f32[6,1,1,128,128]{4,3,2,1,0:T(8,128)}, u32[]{:S(2)}) copy-start(f32[6,1,1,128,128]{4,3,2,1,0:T(8,128)} %param.12) | copy-start | bytes 1179652
  198.7 20.3 %collective-permute-start = (f32[6,128,128]{2,1,0:T(8,128)}, f32[6,128,128]{2,1,0:T(8,128)S(1)}, u32[]{:S(2)}, u32[]{:S(2)}) collective-permute-start(f32[6,128,128]{2,1,0:T(8,128)} %get-tuple-element.79), channel_id=1, source_target_pairs={{24,0},{25,1},{26,2},{27,3},{28,4},{29,5},{30,6},{31,7},{0,8},{1,9... | collective-permute-start | bytes 1179656 | tf_op jit(solution)/shard_map/ppermute | solution.py:10
  198.7 20.3 %collective-permute-start.1 = (f32[6,128,128]{2,1,0:T(8,128)}, f32[6,128,128]{2,1,0:T(8,128)}, u32[]{:S(2)}, u32[]{:S(2)}) collective-permute-start(f32[6,128,128]{2,1,0:T(8,128)} %get-tuple-element.81), channel_id=1, source_target_pairs={{16,0},{17,1},{18,2},{19,3},{20,4},{21,5},{22,6},{23,7},{24,8},{25... | collective-permute-start | bytes 1179656 | tf_op jit(solution)/shard_map/ppermute | solution.py:10
  198.7 20.7 %collective-permute-start.2 = (f32[6,128,128]{2,1,0:T(8,128)S(1)}, f32[6,128,128]{2,1,0:T(8,128)}, u32[]{:S(2)}, u32[]{:S(2)}) collective-permute-start(f32[6,128,128]{2,1,0:T(8,128)S(1)} %get-tuple-element.80), channel_id=1, source_target_pairs={{8,0},{9,1},{10,2},{11,3},{12,4},{13,5},{14,6},{15,7},{16,8},{17,9... | collective-permute-start | bytes 1179656 | tf_op jit(solution)/shard_map/ppermute | solution.py:10
  220.7 0.7 copy-start.2
  221.4 173.0 %all-gather.11.cloned.1.call-start = ((), (), s32[]{:S(2)}) async-start(), calls=%async_computation.5 | async-start | bytes 2359296 | tf_op jit(solution)/shard_map/all_gather | solution.py:15
  365.7 204.1 %all-reduce.9.cloned.1.call-start = ((), (), s32[]{:S(2)}) async-start(), calls=%async_computation.2 | async-start | bytes 524288 | tf_op jit(solution)/shard_map/psum | solution.py:57
  399.4 16.8 %collective-permute-start.3 = (f32[6,128,128]{2,1,0:T(8,128)}, f32[6,128,128]{2,1,0:T(8,128)S(1)}, u32[]{:S(2)}, u32[]{:S(2)}) collective-permute-start(f32[6,128,128]{2,1,0:T(8,128)} %get-tuple-element.76), channel_id=1, source_target_pairs={{24,0},{25,1},{26,2},{27,3},{28,4},{29,5},{30,6},{31,7},{0,8},{1,9... | collective-permute-start | bytes 1179656 | tf_op jit(solution)/shard_map/ppermute | solution.py:10
  407.6 17.0 %collective-permute-start.4 = (f32[6,128,128]{2,1,0:T(8,128)}, f32[6,128,128]{2,1,0:T(8,128)}, u32[]{:S(2)}, u32[]{:S(2)}) collective-permute-start(f32[6,128,128]{2,1,0:T(8,128)} %get-tuple-element.78), channel_id=1, source_target_pairs={{16,0},{17,1},{18,2},{19,3},{20,4},{21,5},{22,6},{23,7},{24,8},{25... | collective-permute-start | bytes 1179656 | tf_op jit(solution)/shard_map/ppermute | solution.py:10
  407.6 18.1 %collective-permute-start.5 = (f32[6,128,128]{2,1,0:T(8,128)S(1)}, f32[6,128,128]{2,1,0:T(8,128)}, u32[]{:S(2)}, u32[]{:S(2)}) collective-permute-start(f32[6,128,128]{2,1,0:T(8,128)S(1)} %get-tuple-element.77), channel_id=1, source_target_pairs={{8,0},{9,1},{10,2},{11,3},{12,4},{13,5},{14,6},{15,7},{16,8},{17,9... | collective-permute-start | bytes 1179656 | tf_op jit(solution)/shard_map/ppermute | solution.py:10
  426.9 0.7 copy-start.3
  427.6 174.1 %all-gather.13.cloned.1.call-start = ((), (), s32[]{:S(2)}) async-start(), calls=%async_computation.6 | async-start | bytes 2359296 | tf_op jit(solution)/shard_map/all_gather | solution.py:15
  573.0 205.7 %all-reduce.11.cloned.1.call-start = ((), (), s32[]{:S(2)}) async-start(), calls=%async_computation.3 | async-start | bytes 524288 | tf_op jit(solution)/shard_map/psum | solution.py:57
  607.0 11.9 %collective-permute-start.6 = (f32[6,128,128]{2,1,0:T(8,128)}, f32[6,128,128]{2,1,0:T(8,128)S(1)}, u32[]{:S(2)}, u32[]{:S(2)}) collective-permute-start(f32[6,128,128]{2,1,0:T(8,128)} %get-tuple-element.73), channel_id=1, source_target_pairs={{24,0},{25,1},{26,2},{27,3},{28,4},{29,5},{30,6},{31,7},{0,8},{1,9... | collective-permute-start | bytes 1179656 | tf_op jit(solution)/shard_map/ppermute | solution.py:10
  608.2 26.6 %collective-permute-start.7 = (f32[6,128,128]{2,1,0:T(8,128)}, f32[6,128,128]{2,1,0:T(8,128)}, u32[]{:S(2)}, u32[]{:S(2)}) collective-permute-start(f32[6,128,128]{2,1,0:T(8,128)} %get-tuple-element.75), channel_id=1, source_target_pairs={{16,0},{17,1},{18,2},{19,3},{20,4},{21,5},{22,6},{23,7},{24,8},{25... | collective-permute-start | bytes 1179656 | tf_op jit(solution)/shard_map/ppermute | solution.py:10
  616.7 18.0 %collective-permute-start.8 = (f32[6,128,128]{2,1,0:T(8,128)}, f32[6,128,128]{2,1,0:T(8,128)}, u32[]{:S(2)}, u32[]{:S(2)}) collective-permute-start(f32[6,128,128]{2,1,0:T(8,128)} %get-tuple-element.74), channel_id=1, source_target_pairs={{8,0},{9,1},{10,2},{11,3},{12,4},{13,5},{14,6},{15,7},{16,8},{17,9... | collective-permute-start | bytes 1179656 | tf_op jit(solution)/shard_map/ppermute | solution.py:10
  618.8 15.9 %copy-start.5 = (f32[6,128,128]{2,1,0:T(8,128)}, f32[6,128,128]{2,1,0:T(8,128)S(1)}, u32[]{:S(2)}) copy-start(f32[6,128,128]{2,1,0:T(8,128)S(1)} %collective-permute-done.6) | copy-start | bytes 1179652
  636.1 0.7 copy-start
  636.9 173.9 %all-gather.15.cloned.1.call-start = ((), (), s32[]{:S(2)}) async-start(), calls=%async_computation.7 | async-start | bytes 2359296 | tf_op jit(solution)/shard_map/all_gather | solution.py:15
  815.8 12.3 %collective-permute-start.10 = (f32[6,128,128]{2,1,0:T(8,128)}, f32[6,128,128]{2,1,0:T(8,128)}, u32[]{:S(2)}, u32[]{:S(2)}) collective-permute-start(f32[6,128,128]{2,1,0:T(8,128)} %get-tuple-element.72), channel_id=1, source_target_pairs={{16,0},{17,1},{18,2},{19,3},{20,4},{21,5},{22,6},{23,7},{24,8},{25... | collective-permute-start | bytes 1179656 | tf_op jit(solution)/shard_map/ppermute | solution.py:10
  818.5 25.1 %collective-permute-start.11 = (f32[6,128,128]{2,1,0:T(8,128)}, f32[6,128,128]{2,1,0:T(8,128)}, u32[]{:S(2)}, u32[]{:S(2)}) collective-permute-start(f32[6,128,128]{2,1,0:T(8,128)} %get-tuple-element.71), channel_id=1, source_target_pairs={{8,0},{9,1},{10,2},{11,3},{12,4},{13,5},{14,6},{15,7},{16,8},{17,9... | collective-permute-start | bytes 1179656 | tf_op jit(solution)/shard_map/ppermute | solution.py:10
  825.2 18.3 %collective-permute-start.9 = (f32[6,128,128]{2,1,0:T(8,128)}, f32[6,128,128]{2,1,0:T(8,128)}, u32[]{:S(2)}, u32[]{:S(2)}) collective-permute-start(f32[6,128,128]{2,1,0:T(8,128)} %get-tuple-element.70), channel_id=1, source_target_pairs={{24,0},{25,1},{26,2},{27,3},{28,4},{29,5},{30,6},{31,7},{0,8},{1,9... | collective-permute-start | bytes 1179656 | tf_op jit(solution)/shard_map/ppermute | solution.py:10
Sparse Core Ops, SparseCore 0:
  12.0 142.6 all-reduce.4
  158.1 28.5 all-gather.8
  221.5 140.8 all-reduce.6
  365.8 28.5 all-gather.10
  427.8 141.9 all-reduce.8
  573.2 28.5 all-gather.12
  637.0 141.7 all-reduce.10
  782.1 28.5 all-gather.14
